TPU v7x, 32 devices: a whole 2x2x4 slice. The times are simulated.
32 devices in a mesh: row: 4 (over y, x), col: 8 (over z, core).
Axes of the slice: x: 2, y: 2, z: 4, core: 2. Of those that a mesh axis runs over, the one named last changes fastest.
Arguments:
- momentum: float32 [4608, 8192], P('row', 'col'), may hold values from -37 to 37
Outputs:
- update: float32 [4608, 8192], P('row', 'col')
All inputs are finite; a program needn't handle non-finite values.
Results may differ from a plain program's by a relative error of at most 0.0049.
Values may be sent and summed in bfloat16 or wider, within the bound.
No kernel may reach another device: no remote copies, remote signals or barrier semaphores. Data moves between devices by JAX's collectives and lax.ppermute only.
A program may use at most 128 MiB of HBM per device.

v0:
```python
import math
import jax
import jax.numpy as jnp
from jax import lax
from jax.sharding import PartitionSpec as P

ROWS = 4608
COLS = 8192
quintic_a = 3.4445
quintic_b = -4.775
quintic_c = 2.0315


def from_root(shard, axis, root):
    mine = lax.axis_index(axis) == root
    return lax.psum(jnp.where(mine, shard, jnp.zeros_like(shard)), axis)


def rows_product(left, right):
    return lax.dot_general(
        left, right, (((1,), (1,)), ((), ())), preferred_element_type=jnp.float32
    )


def body(momentum):
    partial_sum = jnp.sum(momentum * momentum)
    norm_squares = lax.psum(partial_sum, ("row", "col"))
    factor = 0.6 * math.sqrt(ROWS) / (jnp.sqrt(norm_squares) + 1e-07)
    scaled = (momentum * factor).astype(jnp.bfloat16)
    tile_ratio = lax.axis_size("col") // lax.axis_size("row")
    col_index = lax.axis_index("col")
    source_row = col_index // tile_ratio
    half_index = col_index % tile_ratio
    row_panel = lax.all_gather(scaled, "col", axis=1, tiled=True)
    part_rows = row_panel.shape[0] // tile_ratio
    own_part = lax.dynamic_slice_in_dim(row_panel, half_index * part_rows, part_rows, 0)
    peer_rows = from_root(own_part, "row", source_row)
    gram = rows_product(row_panel, peer_rows).astype(jnp.bfloat16)
    gram_panel = lax.all_gather(gram, "col", axis=1, tiled=True)
    gram_columns = lax.all_gather(gram, "row", axis=0, tiled=True)
    squared = jnp.dot(gram_panel, gram_columns, preferred_element_type=jnp.float32)
    poly = (quintic_b * gram.astype(jnp.float32) + quintic_c * squared).astype(jnp.bfloat16)
    poly_panel = lax.all_gather(poly, "col", axis=1, tiled=True)
    product = jnp.dot(
        poly_panel,
        lax.all_gather(scaled, "row", axis=0, tiled=True),
        preferred_element_type=jnp.float32,
    )
    return math.sqrt(COLS) * (quintic_a * scaled.astype(jnp.float32) + product)


def solution(mesh):
    placed = (P("row", "col"),)
    return jax.shard_map(
        body, mesh=mesh, in_specs=placed, out_specs=P("row", "col"), check_vma=False
    )
```

profile of v0, /device:TPU:0, one launch (start us, length us, event | category | flops | bytes accessed | tf_op | source)
XLA Modules:
  0.0 828.4 jit_solution(4937114119938713192)
XLA Ops:
  6.5 4.2 multiply_reduce_fusion
  10.7 42.2 %psum.14 = f32[]{:T(128)} all-reduce(f32[]{:T(128)} %multiply_reduce_fusion), channel_id=1, replica_groups=mesh['row'=4,'col'=8] {'row','col'}, use_global_device_ids=true, to_apply=%region_1.0 | all-reduce | flops 1 | bytes 8 | tf_op jit(solution)/shard_map/psum | solution.py:27
  53.6 4.4 multiply_convert_fusion
  58.0 0.0 all-gather.6.cloned.1.call-update
  58.0 0.0 all-reduce.2.cloned.1.call-start
  58.1 168.3 %all-gather.6.cloned.1.call-done = bf16[1152,8192]{1,0:T(8,128)(2,1)} async-done(((bf16[1152,1024]{1,0:T(8,128)(2,1)}), bf16[1152,8192]{1,0:T(8,128)(2,1)}) %all-gather.6.cloned.1.call-update) | async-done | bytes 18874384 | tf_op jit(solution)/shard_map/all_gather | solution.py:34
  226.5 9.8 %dynamic-slice_select_fusion = bf16[576,8192]{1,0:T(8,128)(2,1)} fusion(bf16[1152,8192]{1,0:T(8,128)(2,1)} %all-gather.6.cloned.1.call-done, s32[]{:T(128)S(6)} %select_n.25, pred[]{:T(512)S(6)} %eq.5), kind=kLoop, calls=%fused_computation | loop fusion | flops 4718592 | bytes 18874372 | tf_op jit(solution)/shard_map/jit(_where)/select_n | solution.py:16
  236.2 0.0 all-reduce.2.cloned.1.call-update
  236.2 0.0 all-gather.10.cloned.1.call-start
  236.3 186.7 %all-reduce.2.cloned.1.call-done = bf16[576,8192]{1,0:T(8,128)(2,1)} async-done(((bf16[576,8192]{1,0:T(8,128)(2,1)}), bf16[576,8192]{1,0:T(8,128)(2,1)}) %all-reduce.2.cloned.1.call-update) | async-done | bytes 9437200 | tf_op jit(solution)/shard_map/psum | solution.py:16
  423.0 18.8 %convolution_convert_fusion = bf16[1152,576]{0,1:T(8,128)(2,1)} fusion(bf16[1152,8192]{1,0:T(8,128)(2,1)} %all-gather.6.cloned.1.call-done, bf16[576,8192]{1,0:T(8,128)(2,1)} %all-reduce.2.cloned.1.call-done), kind=kOutput, calls=%fused_computation.7 | convolution fusion | flops 10872299520 | bytes 29638656 | tf_op jit(solution)/shard_map/dot_general | solution.py:20
  441.8 0.0 all-gather.10.cloned.1.call-update
  441.9 0.0 all-gather.8.cloned.1.call-start
  441.9 0.5 all-gather.8.cloned.1.call-update
  442.4 0.0 all-gather.14.cloned.1.call-start
  442.5 0.5 all-gather.14.cloned.1.call-update
  443.0 0.2 all-gather.12.cloned.1.call-start
  443.3 60.6 %all-gather.10.cloned.1.call-done = bf16[4608,576]{0,1:T(8,128)(2,1)} async-done(((bf16[1152,576]{0,1:T(8,128)(2,1)}), bf16[4608,576]{0,1:T(8,128)(2,1)}) %all-gather.10.cloned.1.call-update) | async-done | bytes 5308432 | tf_op jit(solution)/shard_map/all_gather | solution.py:40
  503.9 102.0 %all-gather.8.cloned.1.call-done = bf16[1152,4608]{0,1:T(8,128)(2,1)} async-done(((bf16[1152,576]{0,1:T(8,128)(2,1)}), bf16[1152,4608]{0,1:T(8,128)(2,1)}) %all-gather.8.cloned.1.call-update) | async-done | bytes 10616848 | tf_op jit(solution)/shard_map/all_gather | solution.py:39
  605.9 13.1 %fusion.2 = bf16[1152,576]{0,1:T(8,128)(2,1)} fusion(bf16[4608,576]{0,1:T(8,128)(2,1)} %all-gather.10.cloned.1.call-done, bf16[1152,4608]{0,1:T(8,128)(2,1)} %all-gather.8.cloned.1.call-done, bf16[1152,576]{0,1:T(8,128)(2,1)} %convolution_convert_fusion), kind=kOutput, calls=%fused_computation.8 | convolution fusion | flops 6118612992 | bytes 18579456 | tf_op jit(solution)/shard_map/dot_general | solution.py:41
  618.9 0.0 all-gather.12.cloned.1.call-update
  619.0 83.1 %all-gather.14.cloned.1.call-done = bf16[4608,1024]{1,0:T(8,128)(2,1)} async-done(((bf16[1152,1024]{1,0:T(8,128)(2,1)}), bf16[4608,1024]{1,0:T(8,128)(2,1)}) %all-gather.14.cloned.1.call-update) | async-done | bytes 9437200 | tf_op jit(solution)/shard_map/all_gather | solution.py:46
  702.1 102.0 %all-gather.12.cloned.1.call-done = bf16[1152,4608]{0,1:T(8,128)(2,1)} async-done(((bf16[1152,576]{0,1:T(8,128)(2,1)}), bf16[1152,4608]{0,1:T(8,128)(2,1)}) %all-gather.12.cloned.1.call-update) | async-done | bytes 10616848 | tf_op jit(solution)/shard_map/all_gather | solution.py:43
  804.1 17.5 %fusion = f32[1152,1024]{1,0:T(8,128)} fusion(bf16[1152,4608]{0,1:T(8,128)(2,1)} %all-gather.12.cloned.1.call-done, bf16[4608,1024]{1,0:T(8,128)(2,1)} %all-gather.14.cloned.1.call-done, bf16[1152,1024]{1,0:T(8,128)(2,1)S(1)} %copy-done), kind=kOutput, calls=%fused_computation.2 | convolution fusion | flops 10876354560 | bytes 27131904 | tf_op jit(solution)/shard_map/dot_general | solution.py:44
  (3 shorter events, 0.0 us)
Async XLA Ops:
  6.5 219.9 %all-gather.6.cloned.1.call-start = ((), (), s32[]{:S(2)}) async-start(), calls=%async_computation | async-start | bytes 21233664 | tf_op jit(solution)/shard_map/all_gather | solution.py:34
  58.0 365.0 %all-reduce.2.cloned.1.call-start = ((), (), s32[]{:S(2)}) async-start(), calls=%async_computation.1 | async-start | bytes 18874368 | tf_op jit(solution)/shard_map/psum | solution.py:16
  236.2 267.6 %all-gather.10.cloned.1.call-start = ((), (), s32[]{:S(2)}) async-start(), calls=%async_computation.3 | async-start | bytes 6635520 | tf_op jit(solution)/shard_map/all_gather | solution.py:40
  441.9 164.0 %all-gather.8.cloned.1.call-start = ((), (), s32[]{:S(2)}) async-start(), calls=%async_computation.2 | async-start | bytes 11943936 | tf_op jit(solution)/shard_map/all_gather | solution.py:39
  442.4 259.7 %all-gather.14.cloned.1.call-start = ((), (), s32[]{:S(2)}) async-start(), calls=%async_computation.5 | async-start | bytes 11796480 | tf_op jit(solution)/shard_map/all_gather | solution.py:46
  443.0 361.1 %copy-start = (bf16[1152,1024]{1,0:T(8,128)(2,1)S(1)}, bf16[1152,1024]{1,0:T(8,128)(2,1)}, u32[]{:S(2)}) copy-start(bf16[1152,1024]{1,0:T(8,128)(2,1)} %multiply_convert_fusion) | copy-start | bytes 7077892
  443.0 361.0 %all-gather.12.cloned.1.call-start = ((), (), s32[]{:S(2)}) async-start(), calls=%async_computation.4 | async-start | bytes 11943936 | tf_op jit(solution)/shard_map/all_gather | solution.py:43
Sparse Core Ops, SparseCore 0:
  58.2 168.2 all-gather.5
  236.4 186.5 all-reduce.1
  442.0 61.8 all-gather.9
  505.4 100.4 all-gather.7
  607.5 94.5 all-gather.13
  703.6 100.4 all-gather.11
where the time goes:
time: 829 us; the launch traced here: 828 us
  waiting for transfers between devices  704 us (85%)
  matrix products  49.4 us (6%)
  blocking collectives  42.2 us (5%)
  other arithmetic  18.3 us (2%)
  between operations  14.2 us (2%)
    psum x1, waiting for transfers between devices, from_root(): return lax.psum(jnp.where(mine, shard, jnp.zeros_like(shard)), axis)  187 us
    all_gather x1, waiting for transfers between devices, body(): row_panel = lax.all_gather(scaled, 'col', axis=1, tiled=True)  168 us
    all_gather x1, waiting for transfers between devices, body(): gram_panel = lax.all_gather(gram, 'col', axis=1, tiled=True)  102 us
    all_gather x1, waiting for transfers between devices, body(): poly_panel = lax.all_gather(poly, 'col', axis=1, tiled=True)  102 us
    all_gather x1, waiting for transfers between devices, body(): lax.all_gather(scaled, 'row', axis=0, tiled=True)  83.1 us
    all_gather x1, waiting for transfers between devices, body(): gram_columns = lax.all_gather(gram, 'row', axis=0, tiled=True)  60.6 us
    psum x1, blocking collectives, body(): norm_squares = lax.psum(partial_sum, ('row', 'col'))  42.2 us
    dot_general x1, matrix products, rows_product(): lax.dot_general(left, right, (((1,), (1,)), ((), ())), preferred_element_...  18.8 us
  transfers between devices with their start and end apart: 6, of which 6 were waited for; matrix products, arithmetic and copies ran while one was open for 2% of the time, Pallas kernels for 0%

commit v1 on v0

--- a/solution.py
+++ b/solution.py
@@ -9,6 +9,27 @@
 quintic_a = 3.4445
 quintic_b = -4.775
 quintic_c = 2.0315
+
+
+def gather_around(array, axis, dim):
+    size, position, rows = (lax.axis_size(axis), lax.axis_index(axis), array.shape[dim])
+    upward = [(i, (i + 1) % size) for i in range(size)]
+    left = [(i, (i - 1) % size) for i in range(size)]
+    filled = jnp.zeros((*array.shape[:dim], size * rows, *array.shape[dim + 1 :]), array.dtype)
+    filled = lax.dynamic_update_slice_in_dim(filled, array, position * rows, axis=dim)
+    from_left = from_right = array
+    halfway = size // 2
+    for step in range(1, halfway + 1):
+        from_left = lax.ppermute(from_left, axis, upward)
+        filled = lax.dynamic_update_slice_in_dim(
+            filled, from_left, (position - step) % size * rows, axis=dim
+        )
+        if step < size - halfway:
+            from_right = lax.ppermute(from_right, axis, left)
+            filled = lax.dynamic_update_slice_in_dim(
+                filled, from_right, (position + step) % size * rows, axis=dim
+            )
+    return filled
 
 
 def from_root(shard, axis, root):
@@ -31,7 +52,7 @@
     col_index = lax.axis_index("col")
     source_row = col_index // tile_ratio
     half_index = col_index % tile_ratio
-    row_panel = lax.all_gather(scaled, "col", axis=1, tiled=True)
+    row_panel = gather_around(scaled, "col", 1)
     part_rows = row_panel.shape[0] // tile_ratio
     own_part = lax.dynamic_slice_in_dim(row_panel, half_index * part_rows, part_rows, 0)
     peer_rows = from_root(own_part, "row", source_row)

time: 829 us -> 861 us (1.039)
  local copies, waits for them, and re-layouts: 0.01 us -> 31.5 us
    all_gather x1 -> x0, waiting for transfers between devices: 168 us -> none  [body(): row_panel = lax.all_gather(scaled, 'col', axis=1, tiled=True)]
    ppermute x0 -> x7, waiting for transfers between devices: none -> 164 us  [the longest x4 164 us: gather_around(): from_left = lax.ppermute(from_left, axis, upward)]
    dynamic_update_slice x0 -> x7, local copies, waits for them, and re-layouts: none -> 21.4 us  [the longest x4 11.6 us: gather_around(): lax.dynamic_update_slice_in_dim(filled, from_left, (position - step) % si...]
  transfers between devices with their start and end apart: 6 -> 12, of which waited for: 6 -> 9; matrix products, arithmetic and copies ran while one was open for 2% -> 4% of each run, Pallas kernels for 0% -> 0%
where the time goes in v1:
time: 861 us
  waiting for transfers between devices  699 us (81%)
  matrix products  49.3 us (6%)
  blocking collectives  42.2 us (5%)
  local copies, waits for them, and re-layouts  31.5 us (4%)
  other arithmetic  16.3 us (2%)
  between operations  13.9 us (2%)
    psum x1, waiting for transfers between devices, from_root(): return lax.psum(jnp.where(mine, shard, jnp.zeros_like(shard)), axis)  187 us
    ppermute x4, waiting for transfers between devices, gather_around(): from_left = lax.ppermute(from_left, axis, upward)  164 us
    all_gather x1, waiting for transfers between devices, body(): gram_panel = lax.all_gather(gram, 'col', axis=1, tiled=True)  102 us
    all_gather x1, waiting for transfers between devices, body(): poly_panel = lax.all_gather(poly, 'col', axis=1, tiled=True)  102 us
    all_gather x1, waiting for transfers between devices, body(): lax.all_gather(scaled, 'row', axis=0, tiled=True)  83.2 us
    all_gather x1, waiting for transfers between devices, body(): gram_columns = lax.all_gather(gram, 'row', axis=0, tiled=True)  60.4 us
    psum x1, blocking collectives, body(): norm_squares = lax.psum(partial_sum, ('row', 'col'))  42.2 us
    dot_general x1, matrix products, rows_product(): lax.dot_general(left, right, (((1,), (1,)), ((), ())), preferred_element_...  18.8 us
  transfers between devices with their start and end apart: 12, of which 9 were waited for; matrix products, arithmetic and copies ran while one was open for 4% of the time, Pallas kernels for 0%

profile of v1, /device:TPU:0, one launch (start us, length us, event | category | flops | bytes accessed | tf_op | source)
XLA Modules:
  0.0 860.9 jit_solution(5462717972462282817)
XLA Ops:
  6.5 4.2 multiply_reduce_fusion
  10.8 42.2 %psum.14 = f32[]{:T(128)} all-reduce(f32[]{:T(128)} %multiply_reduce_fusion), channel_id=1, replica_groups=mesh['row'=4,'col'=8] {'row','col'}, use_global_device_ids=true, to_apply=%region_1.0 | all-reduce | flops 1 | bytes 8 | tf_op jit(solution)/shard_map/psum | solution.py:48
  53.7 7.3 broadcast_in_dim.6
  60.9 2.3 constant_dynamic-update-slice_fusion.7
  63.3 3.5 collective-permute-start.1
  66.8 51.1 %collective-permute-done = bf16[1152,1024]{1,0:T(8,128)(2,1)S(1)} collective-permute-done((bf16[1152,1024]{1,0:T(8,128)(2,1)S(1)}, bf16[1152,1024]{1,0:T(8,128)(2,1)S(1)}, u32[]{:S(2)}, u32[]{:S(2)}) %collective-permute-start) | collective-permute-done | bytes 2359328 | tf_op jit(solution)/shard_map/ppermute | solution.py:23
  121.6 50.7 %collective-permute-done.2 = bf16[1152,1024]{1,0:T(8,128)(2,1)S(1)} collective-permute-done((bf16[1152,1024]{1,0:T(8,128)(2,1)S(1)}, bf16[1152,1024]{1,0:T(8,128)(2,1)S(1)}, u32[]{:S(2)}, u32[]{:S(2)}) %collective-permute-start.2) | collective-permute-done | bytes 2359328 | tf_op jit(solution)/shard_map/ppermute | solution.py:23
  175.9 49.6 %collective-permute-done.4 = bf16[1152,1024]{1,0:T(8,128)(2,1)} collective-permute-done((bf16[1152,1024]{1,0:T(8,128)(2,1)S(1)}, bf16[1152,1024]{1,0:T(8,128)(2,1)}, u32[]{:S(2)}, u32[]{:S(2)}) %collective-permute-start.4) | collective-permute-done | bytes 2359328 | tf_op jit(solution)/shard_map/ppermute | solution.py:23
  225.5 3.4 constant_dynamic-update-slice_fusion.6
  228.9 3.3 constant_dynamic-update-slice_fusion.5
  233.8 3.3 constant_dynamic-update-slice_fusion.3
  237.1 3.3 constant_dynamic-update-slice_fusion.2
  240.4 3.3 constant_dynamic-update-slice_fusion.1
  243.6 12.2 %collective-permute-done.6 = bf16[1152,1024]{1,0:T(8,128)(2,1)} collective-permute-done((bf16[1152,1024]{1,0:T(8,128)(2,1)}, bf16[1152,1024]{1,0:T(8,128)(2,1)}, u32[]{:S(2)}, u32[]{:S(2)}) %collective-permute-start.6) | collective-permute-done | bytes 2359328 | tf_op jit(solution)/shard_map/ppermute | solution.py:23
  255.8 3.3 constant_dynamic-update-slice_fusion
  259.1 9.8 %dynamic-slice_select_fusion = bf16[576,8192]{1,0:T(8,128)(2,1)} fusion(bf16[1152,8192]{1,0:T(8,128)(2,1)} %constant_dynamic-update-slice_fusion, s32[]{:T(128)S(6)} %select_n.92, pred[]{:T(512)S(6)} %eq.12), kind=kLoop, calls=%fused_computation | loop fusion | flops 4718592 | bytes 18874372 | tf_op jit(solution)/shard_map/jit(_where)/select_n | solution.py:37
  269.0 186.8 %all-reduce.2.cloned.1.call-done = bf16[576,8192]{1,0:T(8,128)(2,1)} async-done(((bf16[576,8192]{1,0:T(8,128)(2,1)}), bf16[576,8192]{1,0:T(8,128)(2,1)}) %all-reduce.2.cloned.1.call-update) | async-done | bytes 9437200 | tf_op jit(solution)/shard_map/psum | solution.py:37
  455.7 18.8 %convolution_convert_fusion = bf16[1152,576]{0,1:T(8,128)(2,1)} fusion(bf16[1152,8192]{1,0:T(8,128)(2,1)} %constant_dynamic-update-slice_fusion, bf16[576,8192]{1,0:T(8,128)(2,1)} %all-reduce.2.cloned.1.call-done), kind=kOutput, calls=%fused_computation.6 | convolution fusion | flops 10872299520 | bytes 29638656 | tf_op jit(solution)/shard_map/dot_general | solution.py:41
  476.1 60.4 %all-gather.7.cloned.1.call-done = bf16[4608,576]{0,1:T(8,128)(2,1)} async-done(((bf16[1152,576]{0,1:T(8,128)(2,1)}), bf16[4608,576]{0,1:T(8,128)(2,1)}) %all-gather.7.cloned.1.call-update) | async-done | bytes 5308432 | tf_op jit(solution)/shard_map/all_gather | solution.py:61
  536.6 102.1 %all-gather.5.cloned.1.call-done = bf16[1152,4608]{0,1:T(8,128)(2,1)} async-done(((bf16[1152,576]{0,1:T(8,128)(2,1)}), bf16[1152,4608]{0,1:T(8,128)(2,1)}) %all-gather.5.cloned.1.call-update) | async-done | bytes 10616848 | tf_op jit(solution)/shard_map/all_gather | solution.py:60
  638.7 13.1 %add_convert_fusion = bf16[1152,576]{0,1:T(8,128)(2,1)} fusion(bf16[1152,576]{0,1:T(8,128)(2,1)} %convolution_convert_fusion, bf16[4608,576]{0,1:T(8,128)(2,1)} %all-gather.7.cloned.1.call-done, bf16[1152,4608]{0,1:T(8,128)(2,1)} %all-gather.5.cloned.1.call-done), kind=kOutput, calls=%fused_computation.7 | convolution fusion | flops 6118612992 | bytes 18579456 | tf_op jit(solution)/shard_map/dot_general | solution.py:62
  651.8 83.2 %all-gather.11.cloned.1.call-done = bf16[4608,1024]{1,0:T(8,128)(2,1)} async-done(((bf16[1152,1024]{1,0:T(8,128)(2,1)}), bf16[4608,1024]{1,0:T(8,128)(2,1)}) %all-gather.11.cloned.1.call-update) | async-done | bytes 9437200 | tf_op jit(solution)/shard_map/all_gather | solution.py:67
  735.0 102.0 %all-gather.9.cloned.1.call-done = bf16[1152,4608]{0,1:T(8,128)(2,1)} async-done(((bf16[1152,576]{0,1:T(8,128)(2,1)}), bf16[1152,4608]{0,1:T(8,128)(2,1)}) %all-gather.9.cloned.1.call-update) | async-done | bytes 10616848 | tf_op jit(solution)/shard_map/all_gather | solution.py:64
  836.9 17.5 %fusion = f32[1152,1024]{1,0:T(8,128)} fusion(bf16[1152,4608]{0,1:T(8,128)(2,1)} %all-gather.9.cloned.1.call-done, bf16[4608,1024]{1,0:T(8,128)(2,1)} %all-gather.11.cloned.1.call-done, bf16[1152,1024]{1,0:T(8,128)(2,1)S(1)} %copy-done.1), kind=kOutput, calls=%fused_computation.2 | convolution fusion | flops 10876354560 | bytes 27131904 | tf_op jit(solution)/shard_map/dot_general | solution.py:65
  (37 shorter events, 10.4 us)
Async XLA Ops:
  6.5 449.2 %all-reduce.2.cloned.1.call-start = ((), (), s32[]{:S(2)}) async-start(), calls=%async_computation | async-start | bytes 18874368 | tf_op jit(solution)/shard_map/psum | solution.py:37
  6.5 54.4 %slice-start = ((s8[4718592]{0:T(1024)(128)(4,1)}), s8[524288]{0:T(1024)(128)(4,1)S(1)}, s32[]{:S(2)}) async-start(s8[4718592]{0:T(1024)(128)(4,1)} %bitcast.6), calls=%async_computation.5 | async-start | bytes 1048576
  53.7 7.3 slice-start.1
  63.3 173.8 %copy-start = (bf16[1152,1024]{1,0:T(8,128)(2,1)}, bf16[1152,1024]{1,0:T(8,128)(2,1)S(1)}, u32[]{:S(2)}) copy-start(bf16[1152,1024]{1,0:T(8,128)(2,1)S(1)} %get-tuple-element.6) | copy-start | bytes 7077892
  63.3 54.7 %collective-permute-start = (bf16[1152,1024]{1,0:T(8,128)(2,1)S(1)}, bf16[1152,1024]{1,0:T(8,128)(2,1)S(1)}, u32[]{:S(2)}, u32[]{:S(2)}) collective-permute-start(bf16[1152,1024]{1,0:T(8,128)(2,1)S(1)} %get-tuple-element.6), channel_id=1, source_target_pairs={{0,1},{1,2},{2,3},{3,4},{4,5},{5,6},{6,7},{7,0},{8,9},{9,10},{10,1... | collective-permute-start | bytes 7077896 | tf_op jit(solution)/shard_map/ppermute | solution.py:23
  63.3 54.7 %collective-permute-start.1 = (bf16[1152,1024]{1,0:T(8,128)(2,1)S(1)}, bf16[1152,1024]{1,0:T(8,128)(2,1)S(1)}, u32[]{:S(2)}, u32[]{:S(2)}) collective-permute-start(bf16[1152,1024]{1,0:T(8,128)(2,1)S(1)} %get-tuple-element.6), channel_id=1, source_target_pairs={{0,7},{1,0},{2,1},{3,2},{4,3},{5,4},{6,5},{7,6},{8,15},{9,8},{10,9... | collective-permute-start | bytes 7077896 | tf_op jit(solution)/shard_map/ppermute | solution.py:28
  118.0 1.4 copy-start.2
  118.0 54.3 %collective-permute-start.2 = (bf16[1152,1024]{1,0:T(8,128)(2,1)S(1)}, bf16[1152,1024]{1,0:T(8,128)(2,1)S(1)}, u32[]{:S(2)}, u32[]{:S(2)}) collective-permute-start(bf16[1152,1024]{1,0:T(8,128)(2,1)S(1)} %collective-permute-done), channel_id=1, source_target_pairs={{0,1},{1,2},{2,3},{3,4},{4,5},{5,6},{6,7},{7,0},{8,9},{9,10},{10,1... | collective-permute-start | bytes 7077896 | tf_op jit(solution)/shard_map/ppermute | solution.py:23
  119.4 52.9 %copy-start.3 = (bf16[1152,1024]{1,0:T(8,128)(2,1)}, bf16[1152,1024]{1,0:T(8,128)(2,1)S(1)}, u32[]{:S(2)}) copy-start(bf16[1152,1024]{1,0:T(8,128)(2,1)S(1)} %collective-permute-done.1) | copy-start | bytes 7077892
  119.4 53.0 %collective-permute-start.3 = (bf16[1152,1024]{1,0:T(8,128)(2,1)S(1)}, bf16[1152,1024]{1,0:T(8,128)(2,1)}, u32[]{:S(2)}, u32[]{:S(2)}) collective-permute-start(bf16[1152,1024]{1,0:T(8,128)(2,1)S(1)} %collective-permute-done.1), channel_id=1, source_target_pairs={{0,7},{1,0},{2,1},{3,2},{4,3},{5,4},{6,5},{7,6},{8,15},{9,8},{10,9... | collective-permute-start | bytes 7077896 | tf_op jit(solution)/shard_map/ppermute | solution.py:28
  172.3 1.4 copy-start.4
  172.3 53.2 %collective-permute-start.4 = (bf16[1152,1024]{1,0:T(8,128)(2,1)S(1)}, bf16[1152,1024]{1,0:T(8,128)(2,1)}, u32[]{:S(2)}, u32[]{:S(2)}) collective-permute-start(bf16[1152,1024]{1,0:T(8,128)(2,1)S(1)} %collective-permute-done.2), channel_id=1, source_target_pairs={{0,1},{1,2},{2,3},{3,4},{4,5},{5,6},{6,7},{7,0},{8,9},{9,10},{10,1... | collective-permute-start | bytes 7077896 | tf_op jit(solution)/shard_map/ppermute | solution.py:23
  173.7 66.7 %collective-permute-start.5 = (bf16[1152,1024]{1,0:T(8,128)(2,1)}, bf16[1152,1024]{1,0:T(8,128)(2,1)}, u32[]{:S(2)}, u32[]{:S(2)}) collective-permute-start(bf16[1152,1024]{1,0:T(8,128)(2,1)} %collective-permute-done.3), channel_id=1, source_target_pairs={{0,7},{1,0},{2,1},{3,2},{4,3},{5,4},{6,5},{7,6},{8,15},{9,8},{10,9... | collective-permute-start | bytes 7077896 | tf_op jit(solution)/shard_map/ppermute | solution.py:28
  225.5 30.4 %collective-permute-start.6 = (bf16[1152,1024]{1,0:T(8,128)(2,1)}, bf16[1152,1024]{1,0:T(8,128)(2,1)}, u32[]{:S(2)}, u32[]{:S(2)}) collective-permute-start(bf16[1152,1024]{1,0:T(8,128)(2,1)} %collective-permute-done.4), channel_id=1, source_target_pairs={{0,1},{1,2},{2,3},{3,4},{4,5},{5,6},{6,7},{7,0},{8,9},{9,10},{10,1... | collective-permute-start | bytes 7077896 | tf_op jit(solution)/shard_map/ppermute | solution.py:23
  225.5 6.8 copy-start.5
  268.9 267.6 %all-gather.7.cloned.1.call-start = ((), (), s32[]{:S(2)}) async-start(), calls=%async_computation.2 | async-start | bytes 6635520 | tf_op jit(solution)/shard_map/all_gather | solution.py:61
  474.6 164.1 %all-gather.5.cloned.1.call-start = ((), (), s32[]{:S(2)}) async-start(), calls=%async_computation.1 | async-start | bytes 11943936 | tf_op jit(solution)/shard_map/all_gather | solution.py:60
  475.3 259.7 %all-gather.11.cloned.1.call-start = ((), (), s32[]{:S(2)}) async-start(), calls=%async_computation.4 | async-start | bytes 11796480 | tf_op jit(solution)/shard_map/all_gather | solution.py:67
  475.9 361.1 %copy-start.1 = (bf16[1152,1024]{1,0:T(8,128)(2,1)S(1)}, bf16[1152,1024]{1,0:T(8,128)(2,1)}, u32[]{:S(2)}) copy-start(bf16[1152,1024]{1,0:T(8,128)(2,1)} %copy-done) | copy-start | bytes 7077892
  475.9 361.1 %all-gather.9.cloned.1.call-start = ((), (), s32[]{:S(2)}) async-start(), calls=%async_computation.3 | async-start | bytes 11943936 | tf_op jit(solution)/shard_map/all_gather | solution.py:64
Sparse Core Ops, SparseCore 0:
  269.0 186.6 all-reduce.1
  474.7 61.8 all-gather.6
  538.2 100.4 all-gather.4
  640.4 94.5 all-gather.10
  736.4 100.4 all-gather.8
